TPU v7x, 512 devices: a whole 4x4x16 slice. The times are simulated.
512 devices in a mesh: tm: 8 (over y, core), chan: 64 (over z, x).
Axes of the slice: x: 4, y: 4, z: 16, core: 2. Of those that a mesh axis runs over, the one named last changes fastest.
Arguments:
- spectra: bfloat16 [8, 8192, 8192], P('tm', 'chan'), may hold values from -6 to 6
- block_counts: int32 [64], replicated, may hold values from 1 to 128, 6144 in all
- pairs: int32 [96, 3], replicated, may hold values from 0 to 63, as said below
Outputs:
- stacks: float32 [192, 128, 1024], P('chan', 'tm')
Inputs may be any that keep to these rules, and one draw needn't show every extreme that they name: `pairs`: each owner holds at most 3 pair blocks and some owner holds exactly 3; all pair blocks of one owner share their source block; a target block never equals its source block.
All inputs are finite; a program needn't handle non-finite values.
Results may differ from a plain program's by a relative error of at most 0.0049.
Values may be sent and summed in bfloat16 or wider, within the bound.
A program may use at most 128 MiB of HBM per device.

v0:
```python
import math

import jax
import jax.numpy as jnp
from jax import lax
from jax.sharding import PartitionSpec as P

F = 4096
BAND = 64
LAGS = 8
SLOTS = 3


def phase_tables():
    freq_index = (
        jnp.arange(F // BAND, dtype=jnp.int32)[:, None] * BAND
        + jnp.arange(BAND, dtype=jnp.int32)[None, :]
    )
    lag_values = jnp.arange(LAGS, dtype=jnp.int32) - LAGS // 2
    phase = jnp.mod(lag_values[:, None, None] * freq_index[None], 2 * F)
    angle = jnp.pi * phase.astype(jnp.float32) / F
    return (jnp.cos(angle), jnp.sin(angle))


def whiten(raw, live_count):
    segs, rows, width = raw.shape
    values = raw.astype(jnp.float32).reshape(segs, rows, width // (2 * BAND), 2, BAND)
    power = jnp.mean(values[..., 0, :] ** 2 + values[..., 1, :] ** 2, axis=-1)
    alive = (jnp.arange(rows, dtype=jnp.int32) < live_count).astype(jnp.float32)
    scaled = values * lax.rsqrt(power + 1e-06)[..., None, None] * alive[None, :, None, None, None]
    return scaled.astype(jnp.bfloat16).reshape(segs, rows, width)


def correlate(source, target, cosine, sine, scale):
    groups, segs, rows, width = source.shape
    bands = width // (2 * BAND)
    src = source.reshape(groups, segs, rows, bands, 2, BAND)
    tgt = (
        target.reshape(groups, segs, rows, bands, 2, BAND)
        .transpose(1, 2, 0, 3, 4, 5)
        .astype(jnp.float32)
    )
    real_part = tgt[..., 0, :][:, None]
    imag_part = tgt[..., 1, :][:, None]
    cos_b = cosine.reshape(LAGS, groups, bands, BAND)[None, :, None]
    sin_b = sine.reshape(LAGS, groups, bands, BAND)[None, :, None]
    mod_real = real_part * cos_b + imag_part * sin_b
    mod_imag = imag_part * cos_b - real_part * sin_b
    moved = jnp.stack([mod_real, mod_imag], axis=-2).astype(jnp.bfloat16)
    corr = jnp.einsum("ksiqpf,smjkqpf->imj", src, moved, preferred_element_type=jnp.float32)
    return (corr * scale).reshape(rows, LAGS * rows)


def per_device(spectra, block_counts, pairs):
    chan_count = lax.axis_size("chan")
    my_index = lax.axis_index("chan")
    segs, rows, width = spectra.shape
    scale = 1.0 / math.sqrt(2.0 * F * segs * lax.axis_size("tm"))
    cosine, sine = phase_tables()
    device_ids = jnp.arange(chan_count, dtype=jnp.int32)
    live_count = jnp.sum(jnp.where(device_ids == my_index, block_counts, 0))
    whitened = whiten(spectra, live_count)
    held = lax.all_to_all(whitened[None], "chan", split_axis=3, concat_axis=0, tiled=True)
    owners = pairs[:, 2]
    places = jnp.arange(pairs.shape[0], dtype=jnp.int32)
    earlier = (owners[:, None] == owners[None, :]) & (places[None, :] < places[:, None])
    ranks = jnp.sum(earlier.astype(jnp.int32), axis=1)
    slot_ids = jnp.arange(SLOTS, dtype=jnp.int32)
    matches = (
        (owners[None, None, :] == device_ids[:, None, None])
        & (ranks[None, None, :] == slot_ids[None, :, None])
    ).astype(jnp.int32)
    source_table = jnp.sum(matches * pairs[:, 0][None, None, :], axis=2)
    target_table = jnp.sum(matches * pairs[:, 1][None, None, :], axis=2)
    valid_table = jnp.sum(matches, axis=2)
    my_valid = jnp.sum(jnp.where(device_ids[:, None] == my_index, valid_table, 0), axis=0).astype(
        jnp.float32
    )
    send_source = jnp.take(held, source_table, axis=0)
    send_target = jnp.take(held, target_table, axis=0)
    src_all = lax.all_to_all(send_source, "chan", split_axis=0, concat_axis=0, tiled=True)
    tgt_all = lax.all_to_all(send_target, "chan", split_axis=0, concat_axis=0, tiled=True)

    def one_item(position):
        src_one = lax.dynamic_index_in_dim(src_all, position, 1, False)
        tgt_one = lax.dynamic_index_in_dim(tgt_all, position, 1, False)
        return correlate(src_one, tgt_one, cosine, sine, scale)

    results = lax.map(one_item, jnp.arange(src_all.shape[1], dtype=jnp.int32))
    results = results * my_valid[:, None, None]
    return lax.psum_scatter(results, "tm", scatter_dimension=1, tiled=True)


def solution(mesh):
    placed = (P("tm", "chan", None), P(), P())
    return jax.shard_map(
        per_device, mesh=mesh, in_specs=placed, out_specs=P("chan", "tm", None), check_vma=False
    )
```

profile of v0, /device:TPU:6, one launch (start us, length us, event | category | flops | bytes accessed | tf_op | source)
XLA Modules:
  0.0 956.7 jit_solution(11877595196581559371)
XLA Ops:
  12.8 33.3 %copy.53 = bf16[1,1,128,8192]{2,1,0,3:T(2,128)(2,1)} copy(bf16[1,1,128,8192]{2,3,1,0:T(8,128)(2,1)S(1)} %fusion.21) | data formatting | bytes 4194304 | tf_op jit(solution)/shard_map/convert_element_type | solution.py:31
  46.5 45.2 %reduce.2 = bf16[8192,128]{1,0:T(8,128)(2,1)S(1)} reduce(bf16[8192,1,1,128]{3,2,1,0:T(2,128)(2,1)} %bitcast.78, bf16[]{:T(256)} %broadcast.250), dimensions={1,2}, to_apply=%bitcast.55.reduce_sub_computation | reduce | bytes 4194306
  93.8 18.8 %all-to-all-start = ((bf16[64,2,8192]{2,1,0:T(2,128)(2,1)}), bf16[64,2,8192]{2,1,0:T(2,128)(2,1)S(1)}, u32[]{:S(2)}, u32[]{:S(2)}) async-start(bf16[64,2,8192]{2,1,0:T(2,128)(2,1)} %reshape.305), calls=%async_computation | async-start | bytes 4194304 | tf_op jit(solution)/shard_map/all_to_all | solution.py:63
  113.5 99.3 %all-to-all-done = bf16[64,2,8192]{2,1,0:T(2,128)(2,1)S(1)} async-done(((bf16[64,2,8192]{2,1,0:T(2,128)(2,1)}), bf16[64,2,8192]{2,1,0:T(2,128)(2,1)S(1)}, u32[]{:S(2)}, u32[]{:S(2)}) %all-to-all-start) | async-done | bytes 2097184 | tf_op jit(solution)/shard_map/all_to_all | solution.py:63
  212.7 6.8 reshape.306
  219.5 3.8 copy.50
  226.5 8.0 gather_fusion
  234.5 8.6 copy.37
  243.2 6.1 broadcast_select_fusion
  249.3 6.1 all-to-all-start.1
  255.7 8.0 gather_fusion.1
  263.7 6.0 select_bitcast_fusion
  269.7 265.0 %all-to-all-done.1 = bf16[64,3,1,128,128]{3,4,2,1,0:T(8,128)(2,1)} async-done(((bf16[64,3,1,128,128]{3,4,2,1,0:T(8,128)(2,1)}), bf16[64,3,1,128,128]{3,4,2,1,0:T(8,128)(2,1)}, u32[]{:S(2)}, u32[]{:S(2)}) %all-to-all-start.1) | async-done | bytes 6291488 | tf_op jit(solution)/shard_map/all_to_all | solution.py:81
  534.7 6.1 all-to-all-start.2
  541.9 278.2 %all-to-all-done.2 = bf16[64,3,1,128,128]{4,3,1,2,0:T(8,128)(2,1)} async-done(((bf16[64,3,1,128,128]{4,3,1,2,0:T(8,128)(2,1)}), bf16[64,3,1,128,128]{4,3,1,2,0:T(8,128)(2,1)}, u32[]{:S(2)}, u32[]{:S(2)}) %all-to-all-start.2) | async-done | bytes 6291488 | tf_op jit(solution)/shard_map/all_to_all | solution.py:82
  820.1 94.2 %while.13 = (s32[]{:T(128)}, f32[3,128,1024]{2,1,0:T(8,128)}, s32[3]{0:T(128)S(1)}, bf16[64,3,1,128,128]{3,4,2,1,0:T(8,128)(2,1)}, bf16[64,3,1,128,128]{4,3,1,2,...) while((s32[]{:T(128)}, f32[3,128,1024]{2,1,0:T(8,128)}, ...), condition=%wide.region_6.8_spmd.clone.clone.clone, body=%wide.region_5.7_spmd.clone.clone.clone.sunk | while | flops 2216230912 | bytes 70271672 | solution.py:89
  831.7 9.9 %add_convert_fusion.2 = (bf16[8,128,64,1,64]{1,4,3,0,2:T(8,128)(2,1)S(1)}, bf16[8,128,64,1,64]{1,4,3,0,2:T(8,128)(2,1)S(1)}) fusion(f32[8,64,64]{2,0,1:T(8,128)S(1)} %get-tuple-element.231, f32[128,64,64]{0,2,1:T(8,128)S(1)} %get-tuple-element.232, f32[8,64,64]{2,0,1:T(8,128)S(1)} %get-tuple-element.233, f32[128,64,64]{0,2,1:T(8,128)S(1)} %get-tuple-element.234), kind=kLoop, calls=%fused_computation.9.clone.1 | loop fusion | flops 33554432 | bytes 21233664 | tf_op jit(solution)/shard_map/convert.2
  843.4 7.1 fusion.36
  863.1 9.9 %add_convert_fusion.2 = (bf16[8,128,64,1,64]{1,4,3,0,2:T(8,128)(2,1)S(1)}, bf16[8,128,64,1,64]{1,4,3,0,2:T(8,128)(2,1)S(1)}) fusion(f32[8,64,64]{2,0,1:T(8,128)S(1)} %get-tuple-element.231, f32[128,64,64]{0,2,1:T(8,128)S(1)} %get-tuple-element.232, f32[8,64,64]{2,0,1:T(8,128)S(1)} %get-tuple-element.233, f32[128,64,64]{0,2,1:T(8,128)S(1)} %get-tuple-element.234), kind=kLoop, calls=%fused_computation.9.clone.1 | loop fusion | flops 33554432 | bytes 21233664 | tf_op jit(solution)/shard_map/convert.2
  874.8 7.1 fusion.36
  885.4 3.2 constant_dynamic-slice_fusion.5
  894.5 9.9 %add_convert_fusion.2 = (bf16[8,128,64,1,64]{1,4,3,0,2:T(8,128)(2,1)S(1)}, bf16[8,128,64,1,64]{1,4,3,0,2:T(8,128)(2,1)S(1)}) fusion(f32[8,64,64]{2,0,1:T(8,128)S(1)} %get-tuple-element.231, f32[128,64,64]{0,2,1:T(8,128)S(1)} %get-tuple-element.232, f32[8,64,64]{2,0,1:T(8,128)S(1)} %get-tuple-element.233, f32[128,64,64]{0,2,1:T(8,128)S(1)} %get-tuple-element.234), kind=kLoop, calls=%fused_computation.9.clone.1 | loop fusion | flops 33554432 | bytes 21233664 | tf_op jit(solution)/shard_map/convert.2
  906.2 7.1 fusion.36
  917.3 32.6 %reduce-scatter.2.cloned.1.call-done = f32[3,16,1024]{2,1,0:T(8,128)} async-done(((f32[3,128,1024]{2,1,0:T(8,128)}), f32[3,16,1024]{2,1,0:T(8,128)}) %reduce-scatter.2.cloned.1.call-update) | async-done | bytes 196624 | tf_op jit(solution)/shard_map/reduce_scatter | solution.py:91
  (66 shorter events, 51.4 us)
Async XLA Ops:
  9.8 1.1 copy-start.1
  91.7 20.9 %copy-start = (s32[96,3]{0,1:T(4,128)S(1)}, s32[96,3]{0,1:T(4,128)}, u32[]{:S(2)}) copy-start(s32[96,3]{0,1:T(4,128)} %param.9) | copy-start | bytes 3460
  93.8 118.9 %all-to-all-start = ((bf16[64,2,8192]{2,1,0:T(2,128)(2,1)}), bf16[64,2,8192]{2,1,0:T(2,128)(2,1)S(1)}, u32[]{:S(2)}, u32[]{:S(2)}) async-start(bf16[64,2,8192]{2,1,0:T(2,128)(2,1)} %reshape.305), calls=%async_computation | async-start | bytes 4194304 | tf_op jit(solution)/shard_map/all_to_all | solution.py:63
  249.3 285.4 %all-to-all-start.1 = ((bf16[64,3,1,128,128]{3,4,2,1,0:T(8,128)(2,1)}), bf16[64,3,1,128,128]{3,4,2,1,0:T(8,128)(2,1)}, u32[]{:S(2)}, u32[]{:S(2)}) async-start(bf16[64,3,1,128,128]{3,4,2,1,0:T(8,128)(2,1)} %broadcast_select_fusion), calls=%async_computation.1 | async-start | bytes 12582912 | tf_op jit(solution)/shard_map/all_to_all | solution.py:81
  534.7 285.4 %all-to-all-start.2 = ((bf16[64,3,1,128,128]{4,3,1,2,0:T(8,128)(2,1)}), bf16[64,3,1,128,128]{4,3,1,2,0:T(8,128)(2,1)}, u32[]{:S(2)}, u32[]{:S(2)}) async-start(bf16[64,3,1,128,128]{4,3,1,2,0:T(8,128)(2,1)} %select_bitcast_fusion), calls=%async_computation.2 | async-start | bytes 12582912 | tf_op jit(solution)/shard_map/all_to_all | solution.py:82
  540.8 409.1 %reduce-scatter.2.cloned.1.call-start = ((), (), s32[]{:S(2)}) async-start(), calls=%async_computation.4 | async-start | bytes 1769472 | tf_op jit(solution)/shard_map/reduce_scatter | solution.py:91
Sparse Core Ops, SparseCore 0:
  917.4 32.4 reduce-scatter.1
where the time goes:
time: 958 us; the launch traced here: 957 us
  waiting for transfers between devices  675 us (70%)
  local copies, waits for them, and re-layouts  109 us (11%)
  other arithmetic  101 us (11%)
  starting transfers between devices  31.2 us (3%)
  matrix products  21.4 us (2%)
  between operations  13.6 us (1%)
    all_to_all x1, waiting for transfers between devices, per_device(): lax.all_to_all(send_target, 'chan', split_axis=0, concat_axis=0, tiled=True)  278 us
    all_to_all x1, waiting for transfers between devices, per_device(): lax.all_to_all(send_source, 'chan', split_axis=0, concat_axis=0, tiled=True)  265 us
    all_to_all x1, waiting for transfers between devices, per_device(): lax.all_to_all(whitened[None], 'chan', split_axis=3, concat_axis=0, tiled...  99.3 us
    unnamed x1, other arithmetic  45.2 us
    convert_element_type x1, local copies, waits for them, and re-layouts, whiten(): return scaled.astype(jnp.bfloat16).reshape(segs, rows, width)  33.3 us
    reduce_scatter x1, waiting for transfers between devices, per_device(): return lax.psum_scatter(results, 'tm', scatter_dimension=1, tiled=True)  32.6 us
    another operation x3, other arithmetic  29.7 us
    dot_general x3, matrix products, correlate(): jnp.einsum('ksiqpf,smjkqpf->imj', src, moved, preferred_element_type=jnp....  21.4 us
  transfers between devices with their start and end apart: 4, of which 4 were waited for; matrix products, arithmetic and copies ran while one was open for 2% of the time, Pallas kernels for 0%

commit v1 on v0

v1 whole, which is shorter than its diff:
```python
import functools

import jax
import jax.numpy as jnp
from jax import lax
from jax.experimental import pallas as pl
from jax.experimental.pallas import tpu as pltpu
from jax.sharding import PartitionSpec as P

F = 4096
BAND = 64
BLK = 128
LAGS = 8
SLOTS = 3
NBLK = 64
NPAIRS = 96
SCALE = 1.0 / 256.0
MESH = pl.DeviceIdType.MESH

NZ, NX, NY = 16, 4, 4
BANDS = F // BAND // NZ
WIDE = 2 * BAND
HALF = 12
MINE = 2 * HALF
BF16 = jnp.bfloat16
F32 = jnp.float32


def place():
    tm, chan = lax.axis_index("tm"), lax.axis_index("chan")
    return tm // 2, tm % 2, chan // NX, chan % NX


def remote(src, dst, send, recv, where):
    return pltpu.make_async_remote_copy(
        src_ref=src, dst_ref=dst, send_sem=send, recv_sem=recv, device_id=where, device_id_type=MESH
    )


def signal_all(barrier, wheres):
    for where in wheres:
        pl.semaphore_signal(barrier, inc=1, device_id=where, device_id_type=MESH)
    pl.semaphore_wait(barrier, len(wheres))


def spread(spec, held, zsend, zrecv, xsend, xrecv, local):
    _, _, z, x = place()
    right = {"chan": z * NX + (x + 1) % NX}
    left = {"chan": z * NX + (x + NX - 1) % NX}
    xl, xr = (x + NX - 1) % NX, (x + 1) % NX

    order = [NZ // 2] + [d for k in range(NZ // 2 - 1, 0, -1) for d in (k, NZ - k)]
    signal_all(
        pltpu.get_barrier_semaphore(),
        [{"chan": (z + d) % NZ * NX + x} for d in range(1, NZ)] + [left, right],
    )

    def columns(zt, q):
        return spec.at[0, :, pl.ds(pl.multiple_of((zt * BANDS + q) * WIDE, WIDE), WIDE)]

    for q in range(BANDS):
        for d in order:
            zt = (z + d) % NZ
            remote(
                columns(zt, q), held.at[q, x, z], zsend.at[q], zrecv.at[q], {"chan": zt * NX + x}
            ).start()
        pltpu.make_async_copy(columns(z, q), held.at[q, x, z], local.at[q]).start()

    rest = NZ - 1
    half = NZ // 2

    def xcopies(q):
        own = held.at[q, x]
        return (remote(own, own, xsend.at[q, 0], xrecv.at[q, 0], right),
                remote(own, own, xsend.at[q, 1], xrecv.at[q, 1], left))

    def fcopies(q):
        lo = held.at[q, xl, pl.ds(0, half)]
        hi = held.at[q, xr, pl.ds(half, half)]
        return (remote(lo, lo, xsend.at[q, 2], xrecv.at[q, 2], right),
                remote(hi, hi, xsend.at[q, 3], xrecv.at[q, 3], left))

    def forward(q):
        a, b = xcopies(q)
        a.wait_recv()
        fcopies(q)[0].start()
        b.wait_recv()
        fcopies(q)[1].start()

    for q in range(BANDS):
        pltpu.make_async_copy(columns(z, q), held.at[q, x, z], local.at[q]).wait()
        got = held.at[q, x, pl.ds(0, rest)]
        pltpu.make_async_copy(got, got, zrecv.at[q]).wait()
        for c in xcopies(q):
            c.start()
        if q:
            forward(q - 1)
    forward(BANDS - 1)
    for q in range(BANDS):
        got = held.at[q, x, pl.ds(0, rest)]
        pltpu.make_async_copy(got, got, zsend.at[q]).wait()
        for c in xcopies(q):
            c.wait_send()
        for c in fcopies(q):
            c.wait_send()
            c.wait_recv()


def call_spread(spectra):
    return pl.pallas_call(
        spread,
        out_shape=jax.ShapeDtypeStruct((BANDS, NX, NZ, BLK, WIDE), BF16),
        in_specs=[pl.BlockSpec(memory_space=pltpu.VMEM)],
        out_specs=pl.BlockSpec(memory_space=pl.ANY),
        scratch_shapes=[
            pltpu.SemaphoreType.DMA((BANDS,)),
            pltpu.SemaphoreType.DMA((BANDS,)),
            pltpu.SemaphoreType.DMA((BANDS, 4)),
            pltpu.SemaphoreType.DMA((BANDS, 4)),
            pltpu.SemaphoreType.DMA((BANDS,)),
        ],
        compiler_params=pltpu.CompilerParams(collective_id=0, has_side_effects=True),
        name="spread",
    )(spectra)


def correlate(table, counts, held, cosine, sine, out, white, moved):
    step = pl.program_id(0)

    @pl.when(step == 0)
    def _():
        lane_row = lax.broadcasted_iota(jnp.int32, (BLK, WIDE), 0)

        def one(zs, carry):
            for xs in range(NX):
                alive = (lane_row < counts[zs * NX + xs]).astype(F32)
                for q in range(BANDS):
                    v = held[q, xs, zs].astype(F32)
                    power = jnp.sum(v * v, axis=-1, keepdims=True) * (1.0 / BAND)
                    scaled = v * lax.rsqrt(power + 1e-06) * alive
                    white[zs * NX + xs, :, q * WIDE : (q + 1) * WIDE] = scaled.astype(BF16)
            return carry

        lax.fori_loop(0, NZ, one, 0)

    source, target = table[0, step], table[1, step]
    for q in range(BANDS):
        cols = slice(q * WIDE, (q + 1) * WIDE)
        v = white[target, :, cols].astype(F32)
        w = pltpu.roll(v, BAND, 1)
        for m in range(LAGS):
            c = cosine[q, m : m + 1, :]
            s = sine[q, m : m + 1, :]
            moved[m * BLK : (m + 1) * BLK, cols] = (v * c + w * s).astype(BF16)
    corr = lax.dot_general(
        white[source], moved[...], (((1,), (1,)), ((), ())), preferred_element_type=F32
    )
    out[0] = (corr * SCALE).astype(BF16)


def call_correlate(table, counts, held, cosine, sine):
    whole = lambda *_: (0,) * 5
    return pl.pallas_call(
        correlate,
        out_shape=jax.ShapeDtypeStruct((MINE, BLK, LAGS * BLK), BF16),
        grid_spec=pltpu.PrefetchScalarGridSpec(
            num_scalar_prefetch=2,
            grid=(MINE,),
            in_specs=[
                pl.BlockSpec((BANDS, NX, NZ, BLK, WIDE), whole, pipeline_mode=pl.Buffered(1)),
                pl.BlockSpec((BANDS, LAGS, WIDE), lambda *_: (0, 0, 0)),
                pl.BlockSpec((BANDS, LAGS, WIDE), lambda *_: (0, 0, 0)),
            ],
            out_specs=pl.BlockSpec((1, BLK, LAGS * BLK), lambda i, *_: (i, 0, 0)),
            scratch_shapes=[
                pltpu.VMEM((NBLK, BLK, BANDS * WIDE), BF16),
                pltpu.VMEM((LAGS * BLK, BANDS * WIDE), BF16),
            ],
        ),
        compiler_params=pltpu.CompilerParams(vmem_limit_bytes=48 << 20),
        name="correlate",
    )(table, counts, held, cosine, sine)


ROWS = 16
TILE = 128
SUB = 2
SUBN = HALF // SUB


def collect(
    part, sends, takes, out,
    mine, other, h, u, v, sums, cp, cm, final, give, got,
    lsem, csend, crecv, ysend, yrecv, psend, precv, msend, mrecv, gsend, grecv,
):
    y, c, z, x = place()
    tm, chan = lax.axis_index("tm"), lax.axis_index("chan")
    core = {"tm": y * 2 + 1 - c}
    up, down = {"tm": (y + 1) % NY * 2 + c}, {"tm": (y + NY - 1) % NY * 2 + c}
    zup, zdown = {"chan": (z + 1) % NZ * NX + x}, {"chan": (z + NZ - 1) % NZ * NX + x}
    owners = NZ * NX

    barrier = pltpu.get_barrier_semaphore()
    for where in (core, up, down):
        pl.semaphore_signal(barrier, inc=1, device_id=where, device_id_type=MESH)

    def greet(d, carry):
        pl.semaphore_signal(
            barrier, inc=1, device_id={"chan": (chan + d) % owners}, device_id_type=MESH
        )
        return carry

    lax.fori_loop(1, owners, greet, 0)
    pl.semaphore_wait(barrier, owners + 2)

    turn = [(y + 2) % NY, (y + 1) % NY, (y + NY - 1) % NY, y]
    swaps = [
        remote(part.at[:, k, 1 - c], other.at[k], csend.at[i], crecv.at[i], core)
        for i, k in enumerate(turn)
    ]
    loads = [
        pltpu.make_async_copy(part.at[:, k, c], mine.at[k], lsem.at[i]) for i, k in enumerate(turn)
    ]
    for a, b in zip(swaps, loads):
        a.start()
        b.start()

    def add_swap(i):
        loads[i].wait()
        swaps[i].wait_recv()
        k = turn[i]

        def one(p, carry):
            mine[k, p] = (mine[k, p].astype(F32) + other[k, p].astype(F32)).astype(BF16)
            return carry

        lax.fori_loop(0, MINE, one, 0)

    lo, hi = pl.ds(0, HALF), pl.ds(HALF, HALF)
    y2, yp, ym = turn[0], turn[1], turn[2]
    ycopy = lambda i, src, dst, where: remote(src, dst, ysend.at[i], yrecv.at[i], where)
    far = [ycopy(0, mine.at[y2, lo], h.at[0], up), ycopy(1, mine.at[y2, hi], h.at[1], down)]
    raw = [ycopy(2, mine.at[yp, hi], u.at[0], up), ycopy(3, mine.at[ym, lo], v.at[0], down)]
    near = [ycopy(4, mine.at[yp, lo], u.at[1], up), ycopy(5, mine.at[ym, hi], v.at[1], down)]

    add_swap(0)
    far[0].start()
    far[1].start()
    add_swap(1)
    raw[0].start()
    add_swap(2)
    raw[1].start()
    add_swap(3)

    for i, (k, base) in enumerate(((yp, 0), (ym, HALF))):
        far[i].wait_recv()

        def one(p, carry):
            mine[k, base + p] = (
                mine[k, base + p].astype(F32) + h[i, p].astype(F32)
            ).astype(BF16)
            return carry

        lax.fori_loop(0, HALF, one, 0)
        near[i].start()

    raw[0].wait_recv()
    raw[1].wait_recv()
    near[0].wait_recv()
    near[1].wait_recv()
    for g in range(2):
        a, b = (u.at[1], v.at[0]) if g == 0 else (u.at[0], v.at[1])

        def one(p, carry):
            t = mine[y, g * HALF + p].astype(F32) + a[p].astype(F32) + b[p].astype(F32)
            for l in range(8):
                sums[g * 8 + l, p] = t[:, l * TILE : (l + 1) * TILE]
            return carry

        lax.fori_loop(0, HALF, one, 0)

    def hop(src, dst, send, recv, where):
        return remote(src, dst, send, recv, where)

    ups, downs = NZ // 2, NZ // 2 - 1
    start_up, start_down = (z + ups) % NZ, (z + NZ - downs) % NZ
    pieces = [pl.ds(b * SUBN, SUBN) for b in range(SUB)]

    def chain_up(s, b):
        src = sums.at[start_up, pieces[b]] if s == 0 else cp.at[s - 1, pieces[b]]
        return hop(src, cp.at[s, pieces[b]], psend.at[s, b], precv.at[s, b], zup)

    def chain_down(s, b):
        src = sums.at[start_down, pieces[b]] if s == 0 else cm.at[s - 1, pieces[b]]
        return hop(src, cm.at[s, pieces[b]], msend.at[s, b], mrecv.at[s, b], zdown)

    for b in range(SUB):
        chain_up(0, b).start()
        chain_down(0, b).start()
    for s in range(1, ups):
        for b in range(SUB):
            chain_up(s - 1, b).wait_recv()
            cp[s - 1, pieces[b]] = cp[s - 1, pieces[b]] + sums[(z + ups - s) % NZ, pieces[b]]
            chain_up(s, b).start()
            if s < downs:
                chain_down(s - 1, b).wait_recv()
                cm[s - 1, pieces[b]] = (
                    cm[s - 1, pieces[b]] + sums[(z + NZ - downs + s) % NZ, pieces[b]]
                )
                chain_down(s, b).start()
    for b in range(SUB):
        chain_down(downs - 1, b).wait_recv()
        chain_up(ups - 1, b).wait_recv()
    final[0:HALF] = (sums[z] + cp[ups - 1] + cm[downs - 1]).astype(BF16)
    final[HALF] = jnp.zeros((ROWS, TILE), BF16)

    def fill(o, carry):
        give[o] = final[sends[o]]
        return carry

    lax.fori_loop(0, owners, fill, 0)

    def deliver(d, carry):
        o = (chan + d) % owners
        remote(give.at[o], got.at[chan], gsend, grecv, {"chan": o}).start()
        return carry

    lax.fori_loop(1, owners, deliver, 0)
    got[chan] = give[chan]
    many = pl.ds(0, owners - 1)
    pltpu.make_async_copy(got.at[many], got.at[many], grecv).wait()

    for k in range(SLOTS):
        base, on = takes[0, k], takes[1, k]
        for l in range(8):
            t = got[base + l * NX].astype(F32)
            out[k, :, l * TILE : (l + 1) * TILE] = jnp.where(on > 0, t, 0.0)

    pltpu.make_async_copy(give.at[many], give.at[many], gsend).wait()
    for s in swaps:
        s.wait_send()
    for s in far + raw + near:
        s.wait_send()
    for b in range(SUB):
        for s in range(ups):
            chain_up(s, b).wait_send()
        for s in range(downs):
            chain_down(s, b).wait_send()


def call_collect(part, sends, takes):
    smem = pl.BlockSpec(memory_space=pltpu.SMEM)
    dma = pltpu.SemaphoreType.DMA
    side = (ROWS, LAGS * BLK)
    return pl.pallas_call(
        collect,
        out_shape=jax.ShapeDtypeStruct((SLOTS, ROWS, LAGS * BLK), F32),
        in_specs=[pl.BlockSpec(memory_space=pl.ANY), smem, smem],
        out_specs=pl.BlockSpec(memory_space=pltpu.VMEM),
        scratch_shapes=[
            pltpu.VMEM((NY, MINE, *side), BF16),
            pltpu.VMEM((NY, MINE, *side), BF16),
            pltpu.VMEM((2, HALF, *side), BF16),
            pltpu.VMEM((2, HALF, *side), BF16),
            pltpu.VMEM((2, HALF, *side), BF16),
            pltpu.VMEM((NZ, HALF, ROWS, TILE), F32),
            pltpu.VMEM((NZ // 2, HALF, ROWS, TILE), F32),
            pltpu.VMEM((NZ // 2 - 1, HALF, ROWS, TILE), F32),
            pltpu.VMEM((HALF + 1, ROWS, TILE), BF16),
            pltpu.VMEM((NBLK, ROWS, TILE), BF16),
            pltpu.VMEM((NBLK, ROWS, TILE), BF16),
            dma((NY,)), dma((NY,)), dma((NY,)),
            dma((6,)), dma((6,)),
            dma((NZ // 2, SUB)), dma((NZ // 2, SUB)),
            dma((NZ // 2 - 1, SUB)), dma((NZ // 2 - 1, SUB)),
            dma, dma,
        ],
        compiler_params=pltpu.CompilerParams(
            collective_id=1, has_side_effects=True, vmem_limit_bytes=40 << 20
        ),
        name="collect",
    )(part, sends, takes)


def phase_tables(z):
    band = z * BANDS + jnp.arange(BANDS, dtype=jnp.int32)
    freq = band[:, None, None] * BAND + jnp.arange(BAND, dtype=jnp.int32)[None, None, :]
    lag = jnp.arange(LAGS, dtype=jnp.int32)[None, :, None] - LAGS // 2
    phase = jnp.mod(lag * freq, 2 * F)
    angle = jnp.pi * phase.astype(F32) / F
    c, s = jnp.cos(angle), jnp.sin(angle)
    return jnp.concatenate([c, c], -1), jnp.concatenate([s, -s], -1)


def plans(pairs, chan):
    z, x = chan // NX, chan % NX
    owners = pairs[:, 2]
    places = jnp.arange(NPAIRS, dtype=jnp.int32)
    before = (owners[None, :] < owners[:, None]) | (
        (owners[None, :] == owners[:, None]) & (places[None, :] < places[:, None])
    )
    rank = jnp.sum(before.astype(jnp.int32), axis=1)
    wanted = places[:MINE] % HALF * 8 + places[:MINE] // HALF * 4 + x
    pick = (rank[None, :] == wanted[:, None]).astype(jnp.int32)
    table = jnp.sum(pick[None] * pairs.T[:2, None, :], axis=2)

    ids = jnp.arange(NBLK, dtype=jnp.int32)
    first = jnp.sum((owners[None, :] < ids[:, None]).astype(jnp.int32), axis=1)
    count = jnp.sum((owners[None, :] == ids[:, None]).astype(jnp.int32), axis=1)
    bin_ = z // 8 * 4 + x
    ahead = jnp.mod(bin_ - first, 8)
    sends = jnp.where(ahead < count, (first + ahead) // 8, HALF)

    me = (ids == chan).astype(jnp.int32)
    r = jnp.sum(me * first) + jnp.arange(SLOTS, dtype=jnp.int32)
    on = (jnp.arange(SLOTS, dtype=jnp.int32) < jnp.sum(me * count)).astype(jnp.int32)
    base = r % 8 // 4 * (8 * NX) + r % 4
    return table, sends, jnp.stack([base, on])


def per_device(spectra, block_counts, pairs):
    chan = lax.axis_index("chan")
    cosine, sine = phase_tables(chan // NX)
    table, sends, takes = plans(pairs, chan)
    held = call_spread(spectra)
    part = call_correlate(table, block_counts, held, cosine, sine)
    return call_collect(part.reshape(MINE, NY, 2, ROWS, LAGS * BLK), sends, takes)


def solution(mesh):
    placed = (P("tm", "chan", None), P(), P())
    return jax.shard_map(
        per_device, mesh=mesh, in_specs=placed, out_specs=P("chan", "tm", None), check_vma=False
    )
```

time: 958 us -> 254 us (0.27)
  waiting for transfers between devices: 675 us -> 0 us
  Pallas kernels: 0 us -> 244 us
  local copies, waits for them, and re-layouts: 109 us -> 4.85 us
  other arithmetic: 101 us -> 2.89 us
  starting transfers between devices: 31.2 us -> 0 us
  matrix products: 21.4 us -> 0 us
  between operations: 13.6 us -> 0.08 us
    all_to_all x3 -> x0, waiting for transfers between devices: 642 us -> none  [the longest x1 278 us: per_device(): lax.all_to_all(send_target, 'chan', split_axis=0, concat_axis=0, tiled=True)]
    pallas_call x0 -> x3, Pallas kernels: none -> 244 us  [the longest x1 132 us: call_spread(): pl.pallas_call(spread, out_shape=jax.ShapeDtypeStruct((BANDS, NX, NZ, BLK...]
    unnamed x1 -> x0, other arithmetic: 45.2 us -> none
    convert_element_type x1 -> x0, local copies, waits for them, and re-layouts: 33.3 us -> none  [whiten(): return scaled.astype(jnp.bfloat16).reshape(segs, rows, width)]
    reduce_scatter x1 -> x0, waiting for transfers between devices: 32.6 us -> none  [per_device(): return lax.psum_scatter(results, 'tm', scatter_dimension=1, tiled=True)]
    all_to_all x3 -> x0, starting transfers between devices: 30.9 us -> none  [the longest x1 18.8 us: per_device(): lax.all_to_all(whitened[None], 'chan', split_axis=3, concat_axis=0, tiled...]
    another operation x3 -> x1, other arithmetic: 29.7 us -> 0.01 us  [plans(): return (table, sends, jnp.stack([base, on]))]
    dynamic_slice x12 -> x0, local copies, waits for them, and re-layouts: 26.4 us -> none  [the longest x6 19.3 us: one_item(): tgt_one = lax.dynamic_index_in_dim(tgt_all, position, 1, False)]
  transfers between devices with their start and end apart: 4 -> 0, of which waited for: 4 -> 0; matrix products, arithmetic and copies ran while one was open for 2% -> 0% of each run, Pallas kernels for 0% -> 0%
where the time goes in v1:
time: 254 us; the launch traced here: 252 us
  Pallas kernels  244 us (96%)
  local copies, waits for them, and re-layouts  4.85 us (2%)
  other arithmetic  2.89 us (1%)
    pallas_call x1, Pallas kernels, call_spread(): pl.pallas_call(spread, out_shape=jax.ShapeDtypeStruct((BANDS, NX, NZ, BLK...  132 us
    pallas_call x1, Pallas kernels, call_collect(): pl.pallas_call(collect, out_shape=jax.ShapeDtypeStruct((SLOTS, ROWS, LAGS...  82.8 us
    pallas_call x1, Pallas kernels, call_correlate(): pl.pallas_call(correlate, out_shape=jax.ShapeDtypeStruct((MINE, BLK, LAGS...  29.6 us

profile of v1, /device:TPU:6, one launch (start us, length us, event | category | flops | bytes accessed | tf_op | source)
XLA Modules:
  0.0 252.2 jit_solution(15028825753307902410)
XLA Ops:
  0.0 0.0 copy-start.1
  0.0 0.7 slice_bitcast_fusion
  0.7 0.2 convert_reduce_fusion
  0.9 0.1 convert_reduce_fusion.2
  1.0 0.7 fusion.9
  1.8 0.7 fusion.8
  2.4 0.7 compare_convert_fusion.1
  3.1 0.7 slice.12
  3.8 0.1 iota_add_fusion
  3.9 0.1 compare_convert_fusion
  4.0 0.1 multiply_reduce_fusion.table
  4.1 0.2 fusion.5
  4.2 0.1 pad_maximum_fusion
  4.3 131.9 %spread.1.held = bf16[4,4,16,128,128]{4,3,2,1,0:T(8,128)(2,1)} custom-call(bf16[1,128,8192]{2,1,0:T(8,128)(2,1)} %spec.1), custom_call_target="tpu_custom_call" | custom-call | tf_op jit(solution)/shard_map/spread/pallas_call | solution.py:110
  136.3 0.0 copy-done.1
  136.3 29.6 %correlate.1 = bf16[24,128,1024]{2,1,0:T(8,128)(2,1)} custom-call(s32[2,24]{1,0:T(2,128)S(1)} %multiply_reduce_fusion.table, s32[64]{0:T(128)S(1)} %copy-done.1, bf16[4,4,16,128,128]{4,3,2,1,0:T(8,128)(2,1)} %spread.1.held, f32[4,8,128]{2,1,0:T(8,128)S(1)} %get-tuple-element.13.cosine, f32[4,8,128]{2,1,0:T(8,128)S(1)} %get-tuple-element.14.sine), custom_call_target="tpu_custom_call" | custom-call | tf_op jit(solution)/shard_map/correlate/pallas_call | solution.py:163
  165.9 0.0 copy-start
  165.9 2.8 %copy-done = bf16[24,128,1024]{2,1,0:T(8,128)(2,1)S(1)} copy-done((bf16[24,128,1024]{2,1,0:T(8,128)(2,1)S(1)}, bf16[24,128,1024]{2,1,0:T(8,128)(2,1)}, u32[]{:S(2)}) %copy-start) | copy-done | bytes 6291480
  168.7 82.8 %collect.1 = f32[3,16,1024]{2,1,0:T(8,128)S(1)} custom-call(bf16[24,4,2,16,1024]{4,3,2,1,0:T(8,128)(2,1)S(1)} %bitcast.4, s32[64]{0:T(128)S(1)} %get-tuple-element.11.sends, s32[2,3]{1,0:T(2,128)S(1)} %pad_add_fusion.takes), custom_call_target="tpu_custom_call" | custom-call | tf_op jit(solution)/shard_map/collect/pallas_call | solution.py:355
  251.5 0.7 copy.5
  (5 shorter events, 0.0 us)
Async XLA Ops:
  0.0 136.3 %copy-start.1 = (s32[64]{0:T(128)S(1)}, s32[64]{0:T(128)}, u32[]{:S(2)}) copy-start(s32[64]{0:T(128)} %counts.1) | copy-start | bytes 772
  165.9 2.8 %copy-start = (bf16[24,128,1024]{2,1,0:T(8,128)(2,1)S(1)}, bf16[24,128,1024]{2,1,0:T(8,128)(2,1)}, u32[]{:S(2)}) copy-start(bf16[24,128,1024]{2,1,0:T(8,128)(2,1)} %correlate.1) | copy-start | bytes 18874372

commit v2 on v0

v2 whole, which is shorter than its diff:
```python
import functools

import jax
import jax.numpy as jnp
from jax import lax
from jax.experimental import pallas as pl
from jax.experimental.pallas import tpu as pltpu
from jax.sharding import PartitionSpec as P

F = 4096
BAND = 64
BLK = 128
LAGS = 8
SLOTS = 3
NBLK = 64
NPAIRS = 96
SCALE = 1.0 / 256.0
MESH = pl.DeviceIdType.MESH

NZ, NX, NY = 16, 4, 4
BANDS = F // BAND // NZ
WIDE = 2 * BAND
HALF = 12
MINE = 2 * HALF
BF16 = jnp.bfloat16
F32 = jnp.float32


def place():
    tm, chan = lax.axis_index("tm"), lax.axis_index("chan")
    return tm // 2, tm % 2, chan // NX, chan % NX


def remote(src, dst, send, recv, where):
    return pltpu.make_async_remote_copy(
        src_ref=src, dst_ref=dst, send_sem=send, recv_sem=recv, device_id=where, device_id_type=MESH
    )


ROWS = 16
TILE = 128
PIECES = 2
PIECE = MINE // PIECES
SUBN = HALF // PIECES
GROUPS = ((0, 1, 15, 2), (14, 3, 13, 4), (12, 5, 11, 6), (10, 7, 9, 8))
RELAY = False


def kernel(
    spec, table, counts, cosine, sine, sends, takes, out,
    held, relay, white, moved, acc, part, mine, other, h, u, v, sums, cp, cm, final, give, got,
    local, zsend, zlow, zrecv, rsend, rrecv, rpass, xsend, xrecv, fsend, frecv,
    csend, crecv, ysend, yrecv, psend, precv, msend, mrecv, gsend, grecv,
):
    y, c, z, x = place()
    chan = lax.axis_index("chan")
    owners = NZ * NX
    xl, xr = (x + NX - 1) % NX, (x + 1) % NX
    right, left = {"chan": z * NX + xr}, {"chan": z * NX + xl}
    core = {"tm": y * 2 + 1 - c}
    up, down = {"tm": (y + 1) % NY * 2 + c}, {"tm": (y + NY - 1) % NY * 2 + c}
    zup, zdown = {"chan": (z + 1) % NZ * NX + x}, {"chan": (z + NZ - 1) % NZ * NX + x}

    barrier = pltpu.get_barrier_semaphore()
    for where in (core, up, down):
        pl.semaphore_signal(barrier, inc=1, device_id=where, device_id_type=MESH)

    def greet(d, carry):
        pl.semaphore_signal(
            barrier, inc=1, device_id={"chan": (chan + d) % owners}, device_id_type=MESH
        )
        return carry

    lax.fori_loop(1, owners, greet, 0)
    pl.semaphore_wait(barrier, owners + 2)

    def columns(zt, q, rows=slice(None)):
        return spec.at[0, rows, pl.ds(pl.multiple_of((zt * BANDS + q) * WIDE, WIDE), WIDE)]

    low, high = pl.ds(0, BLK // 2), pl.ds(BLK // 2, BLK // 2)

    def group_of(d):
        return [j for j, g in enumerate(GROUPS) if d in g][0]

    def own(q):
        return pltpu.make_async_copy(columns(z, q), held.at[q, x, z], local.at[q])

    def to_relay(q):
        return remote(columns((z + 8) % NZ, q, high), relay.at[q], rsend.at[q], rrecv.at[q], zdown)

    def from_relay(q):
        return remote(
            relay.at[q], held.at[q, x, (z + 1) % NZ, high], rpass.at[q], zrecv.at[q, 0],
            {"chan": (z + 9) % NZ * NX + x},
        )

    def zsends(q):
        for group in GROUPS:
            for d in group:
                zt = (z + d) % NZ
                where = {"chan": zt * NX + x}
                if d == 8 and RELAY:
                    remote(
                        columns(zt, q, low), held.at[q, x, z, low], zlow.at[q],
                        zrecv.at[q, 0], where,
                    ).start()
                elif d:
                    remote(
                        columns(zt, q), held.at[q, x, z], zsend.at[q],
                        zrecv.at[q, group_of(d)], where,
                    ).start()

    def zwait(q, j):
        n = len(GROUPS[j])
        if j == 0:
            own(q).wait()
            n -= 1
        got_ = held.at[q, x, pl.ds(0, n)]
        pltpu.make_async_copy(got_, got_, zrecv.at[q, j]).wait()

    def xstart(q, j):
        for d in GROUPS[j]:
            blk = held.at[q, x, (z + NZ - d) % NZ]
            remote(blk, blk, xsend.at[q, 0], xrecv.at[q, j, 0], right).start()
            remote(blk, blk, xsend.at[q, 1], xrecv.at[q, j, 1], left).start()

    def forward(q, j):
        n = len(GROUPS[j])
        for side, (xs, where) in enumerate(((xl, right), (xr, left))):
            got_ = held.at[q, xs, pl.ds(0, n)]
            pltpu.make_async_copy(got_, got_, xrecv.at[q, j, side]).wait()
            for d in GROUPS[j][side * 2 : side * 2 + 2]:
                blk = held.at[q, xs, (z + NZ - d) % NZ]
                remote(blk, blk, fsend.at[q, side], frecv.at[q, side], where).start()

    def fwait(q):
        got_ = held.at[q, x, pl.ds(0, NZ // 2)]
        for side in range(2):
            pltpu.make_async_copy(got_, got_, frecv.at[q, side]).wait()

    row = lax.broadcasted_iota(jnp.int32, (BLK, WIDE), 0)

    def whiten(q):
        def one(zs, carry):
            for xs in range(NX):
                b = zs * NX + xs
                alive = (row < counts[b]).astype(F32)
                t = held[q, xs, zs].astype(F32)
                power = jnp.sum(t * t, axis=-1, keepdims=True) * (1.0 / BAND)
                white[b] = (t * lax.rsqrt(power + 1e-06) * alive).astype(BF16)
            return carry

        lax.fori_loop(0, NZ, one, 0)

    def pair(q, p, slot):
        t = white[table[1, p]].astype(F32)
        w = pltpu.roll(t, BAND, 1)
        for m in range(LAGS):
            moved[slot, m * BLK : (m + 1) * BLK] = (
                t * cosine[q, m : m + 1, :] + w * sine[q, m : m + 1, :]
            ).astype(BF16)
        corr = lax.dot_general(
            white[table[0, p]], moved[slot], (((1,), (1,)), ((), ())), preferred_element_type=F32
        )
        if q == 0:
            acc[p] = corr
        elif q < BANDS - 1:
            acc[p] = acc[p] + corr
        else:
            total = ((acc[p] + corr) * SCALE).astype(BF16)
            for r in range(BLK // ROWS):
                part[p, r] = total[r * ROWS : (r + 1) * ROWS]

    def some_pairs(q, first, count):
        def one(i, carry):
            for slot in range(2):
                pair(q, first + i * 2 + slot, slot)
            return carry

        lax.fori_loop(0, count // 2, one, 0)

    if RELAY:
        for q in range(BANDS):
            to_relay(q).start()
    for q in range(BANDS):
        own(q).start()
        zsends(q)
        if RELAY:
            to_relay(q).wait_recv()
            from_relay(q).start()

    third = MINE // 3
    prev = None
    for q in range(BANDS):
        for j in range(len(GROUPS)):
            zwait(q, j)
            xstart(q, j)
            if prev is not None:
                forward(*prev)
            prev = (q, j)
            if q >= 1 and j == 1:
                fwait(q - 1)
                whiten(q - 1)
            elif q >= 1 and j >= 2:
                some_pairs(q - 1, (j - 2) * third, third)
            elif q >= 2 and j == 0:
                some_pairs(q - 2, 2 * third, third)
    forward(*prev)
    some_pairs(BANDS - 2, 2 * third, third)
    fwait(BANDS - 1)
    whiten(BANDS - 1)

    y2, yp, ym = (y + 2) % NY, (y + 1) % NY, (y + NY - 1) % NY
    turn = [y2, yp, ym, y]

    def piece(b):
        return pl.ds(b * PIECE, PIECE)

    def swap(b, i):
        k = turn[i]
        return remote(
            part.at[piece(b), k * 2 + 1 - c], other.at[k, piece(b)],
            csend.at[b, i], crecv.at[b, i], core,
        )

    def add_swap(b, i):
        swap(b, i).wait_recv()
        k = turn[i]

        def one(p, carry):
            mine[k, p] = (part[p, k * 2 + c].astype(F32) + other[k, p].astype(F32)).astype(BF16)
            return carry

        lax.fori_loop(b * PIECE, (b + 1) * PIECE, one, 0)

    nxt, bck = [yp, ym], [ym, yp]
    ahead, behind = [up, down], [down, up]

    def far(b):
        return remote(mine.at[y2, piece(b)], h.at[b], ysend.at[b, 0], yrecv.at[b, 0], ahead[b])

    def raw(b):
        return remote(
            mine.at[bck[b], piece(b)], v.at[b], ysend.at[b, 1], yrecv.at[b, 1], behind[b]
        )

    def near(b):
        return remote(
            mine.at[nxt[b], piece(b)], u.at[b], ysend.at[b, 2], yrecv.at[b, 2], ahead[b]
        )

    def to_far(b):
        add_swap(b, 0)
        far(b).start()
        back = 2 if b == 0 else 1
        add_swap(b, back)
        raw(b).start()
        add_swap(b, 3 - back)
        add_swap(b, 3)

    def to_near(b):
        far(b).wait_recv()
        k = nxt[b]

        def one(p, carry):
            mine[k, b * PIECE + p] = (
                mine[k, b * PIECE + p].astype(F32) + h[b, p].astype(F32)
            ).astype(BF16)
            return carry

        lax.fori_loop(0, PIECE, one, 0)
        near(b).start()

    def to_sums(b):
        raw(b).wait_recv()
        near(b).wait_recv()

        def one(p, carry):
            for g in range(2):
                i = g * SUBN + p
                t = mine[y, b * PIECE + i].astype(F32) + u[b, i].astype(F32) + v[b, i].astype(F32)
                for l in range(8):
                    sums[b, g * 8 + l, p] = t[:, l * TILE : (l + 1) * TILE]
            return carry

        lax.fori_loop(0, SUBN, one, 0)

    ups, downs = NZ // 2, NZ // 2 - 1

    def chain_up(s, b):
        src = sums.at[b, (z + ups) % NZ] if s == 0 else cp.at[b, s - 1]
        return remote(src, cp.at[b, s], psend.at[s, b], precv.at[s, b], zup)

    def chain_down(s, b):
        src = sums.at[b, (z + NZ - downs) % NZ] if s == 0 else cm.at[b, s - 1]
        return remote(src, cm.at[b, s], msend.at[s, b], mrecv.at[s, b], zdown)

    def link(s, b):
        if s:
            chain_up(s - 1, b).wait_recv()
            cp[b, s - 1] = cp[b, s - 1] + sums[b, (z + ups - s) % NZ]
        chain_up(s, b).start()
        if s and s < downs:
            chain_down(s - 1, b).wait_recv()
            cm[b, s - 1] = cm[b, s - 1] + sums[b, (z + NZ - downs + s) % NZ]
        if s < downs:
            chain_down(s, b).start()

    some_pairs(BANDS - 1, 0, PIECE)
    for i in range(NY):
        swap(0, i).start()
    some_pairs(BANDS - 1, PIECE, PIECE)
    for i in (0, 2, 1, 3):
        swap(1, i).start()
    to_far(0)
    to_far(1)
    to_near(0)
    to_near(1)
    to_sums(0)
    link(0, 0)
    to_sums(1)
    link(0, 1)
    for s in range(1, ups):
        for b in range(PIECES):
            link(s, b)
    for b in range(PIECES):
        chain_down(downs - 1, b).wait_recv()
        chain_up(ups - 1, b).wait_recv()
        final[b * SUBN : (b + 1) * SUBN] = (sums[b, z] + cp[b, ups - 1] + cm[b, downs - 1]).astype(
            BF16
        )
    final[HALF] = jnp.zeros((ROWS, TILE), BF16)

    def fill(o, carry):
        give[o] = final[sends[o]]
        return carry

    lax.fori_loop(0, owners, fill, 0)

    def deliver(d, carry):
        o = (chan + d) % owners
        remote(give.at[o], got.at[chan], gsend, grecv, {"chan": o}).start()
        return carry

    lax.fori_loop(1, owners, deliver, 0)
    got[chan] = give[chan]
    many = pl.ds(0, owners - 1)
    pltpu.make_async_copy(got.at[many], got.at[many], grecv).wait()

    for k in range(SLOTS):
        base, on = takes[0, k], takes[1, k]
        for l in range(8):
            t = got[base + l * NX].astype(F32)
            out[k, :, l * TILE : (l + 1) * TILE] = jnp.where(on > 0, t, 0.0)

    pltpu.make_async_copy(give.at[many], give.at[many], gsend).wait()
    for q in range(BANDS):
        sent = held.at[q, x, pl.ds(0, NZ - 1)]
        if RELAY:
            to_relay(q).wait_send()
            from_relay(q).wait_send()
            gone = held.at[q, x, pl.ds(0, NZ - 2)]
            pltpu.make_async_copy(gone, gone, zsend.at[q]).wait()
            gone = held.at[q, x, 0, low]
            pltpu.make_async_copy(gone, gone, zlow.at[q]).wait()
        else:
            pltpu.make_async_copy(sent, sent, zsend.at[q]).wait()
        for side in range(2):
            sent = held.at[q, x]
            pltpu.make_async_copy(sent, sent, xsend.at[q, side]).wait()
            sent = held.at[q, x, pl.ds(0, NZ // 2)]
            pltpu.make_async_copy(sent, sent, fsend.at[q, side]).wait()
    for b in range(PIECES):
        for i in range(NY):
            swap(b, i).wait_send()
        far(b).wait_send()
        raw(b).wait_send()
        near(b).wait_send()
        for s in range(ups):
            chain_up(s, b).wait_send()
        for s in range(downs):
            chain_down(s, b).wait_send()


def call_kernel(spectra, table, counts, cosine, sine, sends, takes):
    smem = pl.BlockSpec(memory_space=pltpu.SMEM)
    vmem = pl.BlockSpec(memory_space=pltpu.VMEM)
    dma = pltpu.SemaphoreType.DMA
    side = (ROWS, LAGS * BLK)
    tile = (SUBN, ROWS, TILE)
    ups = NZ // 2
    return pl.pallas_call(
        kernel,
        out_shape=jax.ShapeDtypeStruct((SLOTS, ROWS, LAGS * BLK), F32),
        in_specs=[vmem, smem, smem, vmem, vmem, smem, smem],
        out_specs=vmem,
        scratch_shapes=[
            pltpu.VMEM((BANDS, NX, NZ, BLK, WIDE), BF16),
            pltpu.VMEM((BANDS, BLK // 2, WIDE), BF16),
            pltpu.VMEM((NBLK, BLK, WIDE), BF16),
            pltpu.VMEM((2, LAGS * BLK, WIDE), BF16),
            pltpu.VMEM((MINE, BLK, LAGS * BLK), F32),
            pltpu.VMEM((MINE, BLK // ROWS, *side), BF16),
            pltpu.VMEM((NY, MINE, *side), BF16),
            pltpu.VMEM((NY, MINE, *side), BF16),
            pltpu.VMEM((PIECES, PIECE, *side), BF16),
            pltpu.VMEM((PIECES, PIECE, *side), BF16),
            pltpu.VMEM((PIECES, PIECE, *side), BF16),
            pltpu.VMEM((PIECES, NZ, *tile), F32),
            pltpu.VMEM((PIECES, ups, *tile), F32),
            pltpu.VMEM((PIECES, ups - 1, *tile), F32),
            pltpu.VMEM((HALF + 1, ROWS, TILE), BF16),
            pltpu.VMEM((NBLK, ROWS, TILE), BF16),
            pltpu.VMEM((NBLK, ROWS, TILE), BF16),
            dma((BANDS,)),
            dma((BANDS,)), dma((BANDS,)), dma((BANDS, 4)),
            dma((BANDS,)), dma((BANDS,)), dma((BANDS,)),
            dma((BANDS, 2)), dma((BANDS, 4, 2)),
            dma((BANDS, 2)), dma((BANDS, 2)),
            dma((PIECES, NY)), dma((PIECES, NY)),
            dma((PIECES, 3)), dma((PIECES, 3)),
            dma((ups, PIECES)), dma((ups, PIECES)),
            dma((ups - 1, PIECES)), dma((ups - 1, PIECES)),
            dma, dma,
        ],
        compiler_params=pltpu.CompilerParams(
            collective_id=0, has_side_effects=True, vmem_limit_bytes=58 << 20
        ),
        name="stack",
    )(spectra, table, counts, cosine, sine, sends, takes)


def phase_tables(z):
    band = z * BANDS + jnp.arange(BANDS, dtype=jnp.int32)
    freq = band[:, None, None] * BAND + jnp.arange(BAND, dtype=jnp.int32)[None, None, :]
    lag = jnp.arange(LAGS, dtype=jnp.int32)[None, :, None] - LAGS // 2
    phase = jnp.mod(lag * freq, 2 * F)
    angle = jnp.pi * phase.astype(F32) / F
    c, s = jnp.cos(angle), jnp.sin(angle)
    return jnp.concatenate([c, c], -1), jnp.concatenate([s, -s], -1)


def plans(pairs, chan):
    z, x = chan // NX, chan % NX
    owners = pairs[:, 2]
    places = jnp.arange(NPAIRS, dtype=jnp.int32)
    before = (owners[None, :] < owners[:, None]) | (
        (owners[None, :] == owners[:, None]) & (places[None, :] < places[:, None])
    )
    rank = jnp.sum(before.astype(jnp.int32), axis=1)
    i = places[:MINE]
    spot = i // (2 * SUBN) * SUBN + i % SUBN
    wanted = spot * 8 + i // SUBN % 2 * 4 + x
    pick = (rank[None, :] == wanted[:, None]).astype(jnp.int32)
    table = jnp.sum(pick[None] * pairs.T[:2, None, :], axis=2)

    ids = jnp.arange(NBLK, dtype=jnp.int32)
    first = jnp.sum((owners[None, :] < ids[:, None]).astype(jnp.int32), axis=1)
    count = jnp.sum((owners[None, :] == ids[:, None]).astype(jnp.int32), axis=1)
    bin_ = z // 8 * 4 + x
    ahead = jnp.mod(bin_ - first, 8)
    sends = jnp.where(ahead < count, (first + ahead) // 8, HALF)

    me = (ids == chan).astype(jnp.int32)
    r = jnp.sum(me * first) + jnp.arange(SLOTS, dtype=jnp.int32)
    on = (jnp.arange(SLOTS, dtype=jnp.int32) < jnp.sum(me * count)).astype(jnp.int32)
    base = r % 8 // 4 * (8 * NX) + r % 4
    return table, sends, jnp.stack([base, on])


def per_device(spectra, block_counts, pairs):
    chan = lax.axis_index("chan")
    cosine, sine = phase_tables(chan // NX)
    table, sends, takes = plans(pairs, chan)
    return call_kernel(spectra, table, block_counts, cosine, sine, sends, takes)


def solution(mesh):
    placed = (P("tm", "chan", None), P(), P())
    return jax.shard_map(
        per_device, mesh=mesh, in_specs=placed, out_specs=P("chan", "tm", None), check_vma=False
    )
```

time: 958 us -> 214 us (0.22)
  waiting for transfers between devices: 675 us -> 0 us
  Pallas kernels: 0 us -> 205 us
  local copies, waits for them, and re-layouts: 109 us -> 2.99 us
  other arithmetic: 101 us -> 5.14 us
  starting transfers between devices: 31.2 us -> 0 us
  matrix products: 21.4 us -> 0 us
  between operations: 13.6 us -> 0.04 us
    all_to_all x3 -> x0, waiting for transfers between devices: 642 us -> none  [the longest x1 278 us: per_device(): lax.all_to_all(send_target, 'chan', split_axis=0, concat_axis=0, tiled=True)]
    pallas_call x0 -> x1, Pallas kernels: none -> 205 us  [call_kernel(): pl.pallas_call(kernel, out_shape=jax.ShapeDtypeStruct((SLOTS, ROWS, LAGS...]
    unnamed x1 -> x0, other arithmetic: 45.2 us -> none
    convert_element_type x1 -> x0, local copies, waits for them, and re-layouts: 33.3 us -> none  [whiten(): return scaled.astype(jnp.bfloat16).reshape(segs, rows, width)]
    reduce_scatter x1 -> x0, waiting for transfers between devices: 32.6 us -> none  [per_device(): return lax.psum_scatter(results, 'tm', scatter_dimension=1, tiled=True)]
    all_to_all x3 -> x0, starting transfers between devices: 30.9 us -> none  [the longest x1 18.8 us: per_device(): lax.all_to_all(whitened[None], 'chan', split_axis=3, concat_axis=0, tiled...]
    another operation x3 -> x1, other arithmetic: 29.7 us -> 0.55 us  [plans(): return (table, sends, jnp.stack([base, on]))]
    dynamic_slice x12 -> x0, local copies, waits for them, and re-layouts: 26.4 us -> none  [the longest x6 19.3 us: one_item(): tgt_one = lax.dynamic_index_in_dim(tgt_all, position, 1, False)]
  transfers between devices with their start and end apart: 4 -> 0, of which waited for: 4 -> 0; matrix products, arithmetic and copies ran while one was open for 2% -> 0% of each run, Pallas kernels for 0% -> 0%
where the time goes in v2:
time: 214 us; the launch traced here: 213 us
  Pallas kernels  205 us (96%)
  other arithmetic  5.14 us (2%)
  local copies, waits for them, and re-layouts  2.99 us (1%)
    pallas_call x1, Pallas kernels, call_kernel(): pl.pallas_call(kernel, out_shape=jax.ShapeDtypeStruct((SLOTS, ROWS, LAGS...  205 us

profile of v2, /device:TPU:6, one launch (start us, length us, event | category | flops | bytes accessed | tf_op | source)
XLA Modules:
  0.0 212.9 jit_solution(16976463542171104160)
XLA Ops:
  0.0 0.7 slice_bitcast_fusion
  0.7 0.2 convert_reduce_fusion
  0.9 0.1 convert_reduce_fusion.2
  1.0 1.3 fusion.10
  2.3 0.7 fusion.9
  3.0 0.7 compare_convert_fusion.1
  3.7 0.5 pad_add_fusion.takes
  4.2 0.7 slice.11
  4.9 0.1 iota_add_fusion
  5.0 0.1 compare_convert_fusion
  5.0 0.7 multiply_reduce_fusion.table
  5.7 0.2 fusion.5
  5.9 0.7 pad_maximum_fusion
  6.5 204.7 %stack.7 = f32[3,16,1024]{2,1,0:T(8,128)} custom-call(bf16[1,128,8192]{2,1,0:T(8,128)(2,1)} %spec.1, s32[2,24]{1,0:T(2,128)} %multiply_reduce_fusion.table, s32[64]{0:T(128)} %counts.1, f32[4,8,128]{2,1,0:T(8,128)} %get-tuple-element.13.cosine, f32[4,8,128]{2,1,0:T(8,128)} %get-tuple-element.14.sine, s32[64]{0:T(128)} %get-tuple-element.11.sends, ...), custom_call_target="tpu_custom_call" | custom-call | tf_op jit(solution)/shard_map/stack/pallas_call | solution.py:392
  211.3 1.6 copy.5
  (4 shorter events, 0.0 us)

commit v3 on v0

v3 whole, which is shorter than its diff:
```python
import jax
import jax.numpy as jnp
import numpy as np
from jax import lax
from jax.experimental import pallas as pl
from jax.experimental.pallas import tpu as pltpu
from jax.sharding import PartitionSpec as P

F = 4096
BAND = 64
BLK = 128
LAGS = 8
SLOTS = 3
NBLK = 64
NPAIRS = 96
SCALE = 1.0 / 256.0
MESH = pl.DeviceIdType.MESH
BF16 = jnp.bfloat16
F32 = jnp.float32

NZ, NX, NY = 16, 4, 4
BANDS = F // BAND // NZ
WIDE = 2 * BAND
MINE = NPAIRS // NX
PIECES = (4, 4, 4, 4, 3, 3, 1, 1)
FIRST = tuple(sum(PIECES[:b]) for b in range(len(PIECES)))
QUAD = 4
ROWS = 16
TROW, TCOL = 8, 128
TALL, FLAT = ROWS // TROW, LAGS * BLK // TCOL

GROUPS = ((0, 1, 15, 2), (14, 3, 13, 4), (12, 5, 11, 6), (10, 7, 9, 8))
LAST = GROUPS[:3] + ((10, 7), (9, 8))


def groups_of(q):
    return LAST if q == BANDS - 1 else GROUPS


def place():
    tm, chan = lax.axis_index("tm"), lax.axis_index("chan")
    return tm // 2, tm % 2, chan // NX, chan % NX


def remote(src, dst, send, recv, where):
    return pltpu.make_async_remote_copy(
        src_ref=src, dst_ref=dst, send_sem=send, recv_sem=recv, device_id=where, device_id_type=MESH
    )


def bytes_of(ref, sem):
    pltpu.make_async_copy(ref, ref, sem).wait()


def kernel(
    spectra, phases, table, ranks, counts, out,
    spec, trig, held0, held1, held2, held3, moved, acc, part, mine, other, h, u, v,
    sums, sent1, got1, sum2, sent2, got2, final, give, got,
    local, zsend, zrecv, xsend, xrecv, fsend, frecv,
    csend, crecv, ysend, yrecv, send1, recv1, send2, recv2, gsend, grecv,
):
    y, c, z, x = place()
    chan = lax.axis_index("chan")
    owners = NZ * NX
    xl, xr = (x + NX - 1) % NX, (x + 1) % NX
    right, left = {"chan": z * NX + xr}, {"chan": z * NX + xl}
    core = {"tm": y * 2 + 1 - c}
    up, down = {"tm": (y + 1) % NY * 2 + c}, {"tm": (y + NY - 1) % NY * 2 + c}
    opposite = {"chan": z * NX + (x + 2) % NX}
    held = (held0, held1, held2, held3)

    def slot(xs, zs):
        return xs * NZ + zs

    def slots(xs, n):
        return pl.ds(xs * NZ, n)

    load = pltpu.make_async_copy(spectra.at[0], spec, local.at[BANDS])
    load.start()
    load_trig = pltpu.make_async_copy(phases.at[z], trig, local.at[BANDS + 1])
    load_trig.start()

    barrier = pltpu.get_barrier_semaphore()
    for where in (core, up, down):
        pl.semaphore_signal(barrier, inc=1, device_id=where, device_id_type=MESH)

    def greet(d, carry):
        pl.semaphore_signal(
            barrier, inc=1, device_id={"chan": (chan + d) % owners}, device_id_type=MESH
        )
        return carry

    lax.fori_loop(1, owners, greet, 0)
    load.wait()
    load_trig.wait()
    alive = (lax.broadcasted_iota(jnp.int32, (BLK, WIDE), 0) < counts[chan]).astype(F32)

    def whiten(i, carry):
        cols = pl.ds(pl.multiple_of(i * WIDE, WIDE), WIDE)
        t = spec[:, cols].astype(F32)
        power = jnp.sum(t * t, axis=-1, keepdims=True) * (1.0 / BAND)
        spec[:, cols] = (t * lax.rsqrt(power + 1e-06) * alive).astype(BF16)
        return carry

    lax.fori_loop(0, F // BAND, whiten, 0)
    pl.semaphore_wait(barrier, owners + 2)

    def columns(zt, q):
        return spec.at[:, pl.ds(pl.multiple_of((zt * BANDS + q) * WIDE, WIDE), WIDE)]

    def own(q):
        return pltpu.make_async_copy(columns(z, q), held[q].at[slot(x, z)], local.at[q])

    def zsends(q):
        for j, group in enumerate(groups_of(q)):
            for d in group:
                if d:
                    zt = (z + d) % NZ
                    remote(
                        columns(zt, q), held[q].at[slot(x, z)], zsend.at[q], zrecv.at[q, j],
                        {"chan": zt * NX + x},
                    ).start()

    def zwait(q, j):
        n = len(groups_of(q)[j])
        if j == 0:
            own(q).wait()
            n -= 1
        bytes_of(held[q].at[slots(x, n)], zrecv.at[q, j])

    def direct(q, j):
        return q == BANDS - 1 and j >= 3

    def xstart(q, j):
        for d in groups_of(q)[j]:
            blk = held[q].at[slot(x, (z + NZ - d) % NZ)]
            remote(blk, blk, xsend.at[q, 0], xrecv.at[q, j, 0], right).start()
            remote(blk, blk, xsend.at[q, 1], xrecv.at[q, j, 1], left).start()
            if direct(q, j):
                remote(blk, blk, fsend.at[q, 2], frecv.at[q, 2], opposite).start()

    def forward(q, j):
        group = groups_of(q)[j]
        n = len(group)
        for side, (xs, where) in enumerate(((xl, right), (xr, left))):
            bytes_of(held[q].at[slots(xs, n)], xrecv.at[q, j, side])
            if not direct(q, j):
                for d in group[side * n // 2 : (side + 1) * n // 2]:
                    blk = held[q].at[slot(xs, (z + NZ - d) % NZ)]
                    remote(blk, blk, fsend.at[q, side], frecv.at[q, side], where).start()

    def passed(q):
        return 6 if q == BANDS - 1 else 8

    def fwait(q):
        for side in range(2):
            bytes_of(held[q].at[slots(x, passed(q))], frecv.at[q, side])
        if q == BANDS - 1:
            bytes_of(held[q].at[slots(x, 4)], frecv.at[q, 2])

    def pair(q, p, slot):
        t = held[q][table[1, p]].astype(F32)
        w = pltpu.roll(t, BAND, 1)
        for m in range(LAGS):
            moved[slot, m * BLK : (m + 1) * BLK] = (
                t * trig[0, q, m : m + 1, :] + w * trig[1, q, m : m + 1, :]
            ).astype(BF16)
        corr = lax.dot_general(
            held[q][table[0, p]], moved[slot], (((1,), (1,)), ((), ())),
            preferred_element_type=F32,
        )
        if q == 0:
            acc[p] = corr
        elif q < BANDS - 1:
            acc[p] = acc[p] + corr
        else:
            acc[p] = (acc[p] + corr) * SCALE
            for k in range(NY):
                part[p, k] = acc[p, rows(k, 1 - c)].astype(BF16)

    def rows(k, core_):
        return pl.ds(pl.multiple_of((k * 2 + core_) * ROWS, ROWS), ROWS)

    def some_pairs(q, first, count):
        def one(i, carry):
            for slot in range(2):
                pair(q, first + i * 2 + slot, slot)
            return carry

        lax.fori_loop(0, count // 2, one, 0)

    for q in range(BANDS):
        own(q).start()
        zsends(q)

    third = MINE // 3
    prev = None
    for q in range(BANDS):
        for j in range(len(groups_of(q))):
            zwait(q, j)
            xstart(q, j)
            if prev is not None:
                forward(*prev)
            prev = (q, j)
            if q and j == 1:
                fwait(q - 1)
                some_pairs(q - 1, 0, third)
            elif q and j == 2:
                some_pairs(q - 1, third, 2 * third)
    end = BANDS - 1
    forward(*prev)
    fwait(end)

    y2, yp, ym = (y + 2) % NY, (y + 1) % NY, (y + NY - 1) % NY
    turn = [y2, yp, ym, y]

    def piece(b):
        return pl.ds(FIRST[b], PIECES[b])

    def swap(b, i):
        k = turn[i]
        return remote(
            part.at[piece(b), k], other.at[k, piece(b)], csend.at[b, i], crecv.at[b, i], core
        )

    def swaps(b):
        for i in range(NY):
            swap(b, i).start()

    def add_swap(b, i):
        swap(b, i).wait_recv()
        k = turn[i]

        def one(p, carry):
            mine[k, p] = (acc[p, rows(k, c)] + other[k, p].astype(F32)).astype(BF16)
            return carry

        lax.fori_loop(FIRST[b], FIRST[b] + PIECES[b], one, 0)

    nxt, bck = [yp, ym], [ym, yp]
    ahead, behind = [up, down], [down, up]

    def far(b):
        return remote(mine.at[y2, piece(b)], h.at[piece(b)], ysend.at[b, 0], yrecv.at[b, 0], ahead[b % 2])

    def raw(b):
        return remote(
            mine.at[bck[b % 2], piece(b)], v.at[piece(b)], ysend.at[b, 1], yrecv.at[b, 1], behind[b % 2]
        )

    def near(b):
        return remote(
            mine.at[nxt[b % 2], piece(b)], u.at[piece(b)], ysend.at[b, 2], yrecv.at[b, 2], ahead[b % 2]
        )

    def to_far(b):
        add_swap(b, 0)
        far(b).start()
        back = 2 - b % 2
        add_swap(b, back)
        raw(b).start()
        add_swap(b, 3 - back)
        add_swap(b, 3)

    def to_near(b):
        far(b).wait_recv()
        k = nxt[b % 2]

        def one(p, carry):
            mine[k, p] = (mine[k, p].astype(F32) + h[p].astype(F32)).astype(BF16)
            return carry

        lax.fori_loop(FIRST[b], FIRST[b] + PIECES[b], one, 0)
        near(b).start()

    four, at = z // QUAD, z % QUAD

    def near_z(b, k):
        m = (at + k) % QUAD
        return remote(
            sent1.at[m, :, piece(b)], got1.at[k - 1, :, piece(b)], send1.at[b, k - 1],
            recv1.at[b, k - 1], {"chan": (four * QUAD + m) * NX + x},
        )

    def far_z(b, k):
        f = (four + k) % QUAD
        return remote(
            sent2.at[f, piece(b)], got2.at[k - 1, piece(b)], send2.at[b, k - 1],
            recv2.at[b, k - 1], {"chan": (f * QUAD + at) * NX + x},
        )

    def to_sums(b):
        raw(b).wait_recv()
        near(b).wait_recv()

        def one(p, carry):
            t = mine[y, p].astype(F32) + u[p].astype(F32) + v[p].astype(F32)
            for i in range(NZ):
                r, l = i // FLAT, i % FLAT
                tile = t[r * TROW : (r + 1) * TROW, l * TCOL : (l + 1) * TCOL]
                sums[i % QUAD, i // QUAD, p] = tile
                sent1[i % QUAD, i // QUAD, p] = tile.astype(BF16)
            return carry

        lax.fori_loop(FIRST[b], FIRST[b] + PIECES[b], one, 0)
        for k in range(1, QUAD):
            near_z(b, k).start()

    def to_far_z(b):
        for k in range(1, QUAD):
            near_z(b, k).wait_recv()
        for f in range(QUAD):
            t = sums[at, f, piece(b)]
            for k in range(QUAD - 1):
                t = t + got1[k, f, piece(b)].astype(F32)
            sum2[f, piece(b)] = t
            sent2[f, piece(b)] = t.astype(BF16)
        for k in range(1, QUAD):
            far_z(b, k).start()

    def to_final(b):
        t = sum2[four, piece(b)]
        for k in range(1, QUAD):
            far_z(b, k).wait_recv()
            t = t + got2[k - 1, piece(b)].astype(F32)
        final[piece(b)] = t.astype(final.dtype)

    def both(stage, *couples):
        for g in couples:
            stage(2 * g)
            stage(2 * g + 1)

    def compute(b):
        some_pairs(end, FIRST[b], PIECES[b] + PIECES[b + 1])
        swaps(b)
        swaps(b + 1)

    compute(0)
    compute(2)
    both(to_far, 0)
    compute(4)
    compute(6)
    both(to_near, 0)
    both(to_far, 1)
    both(to_sums, 0)
    both(to_near, 1)
    both(to_far, 2)
    both(to_far_z, 0)
    both(to_sums, 1)
    both(to_near, 2)
    both(to_far, 3)
    both(to_far_z, 1)
    both(to_sums, 2)
    both(to_near, 3)
    both(to_far_z, 2)
    both(to_sums, 3)
    both(to_far_z, 3)
    both(to_final, 0, 1, 2, 3)
    final[MINE] = jnp.zeros((TROW, TCOL), final.dtype)

    def fill(o):
        first = ranks[NPAIRS + o]
        count = ranks[NPAIRS + o + 1] - first
        skip = (x + 4 * NPAIRS - first) % NX
        give[o] = final[jnp.where(skip < count, (first + skip) // NX, MINE)]

    def deliver(d, carry):
        o = (chan + d) % owners
        fill(o)
        remote(give.at[o], got.at[chan], gsend, grecv, {"chan": o}).start()
        return carry

    lax.fori_loop(1, owners, deliver, 0)
    fill(chan)
    got[chan] = give[chan]
    many = pl.ds(0, owners - 1)
    bytes_of(got.at[many], grecv)

    first = ranks[NPAIRS + chan]
    count = ranks[NPAIRS + chan + 1] - first
    for k in range(SLOTS):
        group = (first + k) % NX
        for r in range(TALL):
            for l in range(FLAT):
                t = got[(r * FLAT + l) * NX + group].astype(F32)
                out[k, r * TROW : (r + 1) * TROW, l * TCOL : (l + 1) * TCOL] = jnp.where(
                    k < count, t, 0.0
                )

    bytes_of(give.at[many], gsend)
    for q in range(BANDS):
        bytes_of(held[q].at[slots(x, NZ - 1)], zsend.at[q])
        for side in range(2):
            bytes_of(held[q].at[slots(x, NZ)], xsend.at[q, side])
            bytes_of(held[q].at[slots(x, passed(q))], fsend.at[q, side])
        if q == BANDS - 1:
            bytes_of(held[q].at[slots(x, 4)], fsend.at[q, 2])
    for b in range(len(PIECES)):
        for i in range(NY):
            swap(b, i).wait_send()
        far(b).wait_send()
        raw(b).wait_send()
        near(b).wait_send()
        for k in range(1, QUAD):
            near_z(b, k).wait_send()
            far_z(b, k).wait_send()


def call_kernel(spectra, phases, table, ranks, counts):
    smem = pl.BlockSpec(memory_space=pltpu.SMEM)
    vmem = pl.BlockSpec(memory_space=pltpu.VMEM)
    hbm = pl.BlockSpec(memory_space=pl.ANY)
    dma = pltpu.SemaphoreType.DMA
    side = (ROWS, LAGS * BLK)
    tiles = (QUAD, MINE, TROW, TCOL)
    block = pltpu.VMEM((NBLK, BLK, WIDE), BF16)
    n = len(PIECES)
    return pl.pallas_call(
        kernel,
        out_shape=jax.ShapeDtypeStruct((SLOTS, ROWS, LAGS * BLK), F32),
        in_specs=[hbm, hbm, smem, smem, smem],
        out_specs=vmem,
        scratch_shapes=[
            pltpu.VMEM((BLK, 2 * F), BF16),
            pltpu.VMEM((2, BANDS, LAGS, WIDE), F32),
            block, block, block, block,
            pltpu.VMEM((2, LAGS * BLK, WIDE), BF16),
            pltpu.VMEM((MINE, BLK, LAGS * BLK), F32),
            pltpu.VMEM((MINE, NY, *side), BF16),
            pltpu.VMEM((NY, MINE, *side), BF16),
            pltpu.VMEM((NY, MINE, *side), BF16),
            pltpu.VMEM((MINE, *side), BF16),
            pltpu.VMEM((MINE, *side), BF16),
            pltpu.VMEM((MINE, *side), BF16),
            pltpu.VMEM((QUAD, *tiles), F32),
            pltpu.VMEM((QUAD, *tiles), BF16),
            pltpu.VMEM((QUAD - 1, *tiles), BF16),
            pltpu.VMEM(tiles, F32),
            pltpu.VMEM(tiles, BF16),
            pltpu.VMEM((QUAD - 1, *tiles[1:]), BF16),
            pltpu.VMEM((MINE + 1, TROW, TCOL), BF16),
            pltpu.VMEM((NBLK, TROW, TCOL), BF16),
            pltpu.VMEM((NBLK, TROW, TCOL), BF16),
            dma((BANDS + 2,)),
            dma((BANDS,)), dma((BANDS, 5)),
            dma((BANDS, 2)), dma((BANDS, 5, 2)),
            dma((BANDS, 3)), dma((BANDS, 3)),
            dma((n, NY)), dma((n, NY)),
            dma((n, 3)), dma((n, 3)),
            dma((n, QUAD - 1)), dma((n, QUAD - 1)),
            dma((n, QUAD - 1)), dma((n, QUAD - 1)),
            dma, dma,
        ],
        compiler_params=pltpu.CompilerParams(
            collective_id=0, has_side_effects=True, vmem_limit_bytes=58 << 20
        ),
        name="stack",
    )(spectra, phases, table, ranks, counts)


def phase_tables():
    freq = np.arange(F, dtype=np.int32).reshape(NZ, BANDS, 1, BAND)
    lag = np.arange(LAGS, dtype=np.int32)[:, None] - LAGS // 2
    phase = np.mod(lag * freq, 2 * F)
    angle = np.float32(np.pi) * phase.astype(np.float32) / np.float32(F)
    c, s = np.cos(angle), np.sin(angle)
    return np.stack([np.concatenate([c, c], -1), np.concatenate([s, -s], -1)], axis=1)


def plans(pairs, x):
    places = jnp.arange(NPAIRS, dtype=jnp.int32)
    keys = pairs[:, 2] * NPAIRS + places
    asked = jnp.concatenate([keys, jnp.arange(NBLK + 1, dtype=jnp.int32) * NPAIRS])
    ranks = jnp.sum((keys[None, :] < asked[:, None]).astype(jnp.int32), axis=1)
    wanted = places[:MINE] * NX + x
    pick = (ranks[None, :NPAIRS] == wanted[:, None]).astype(jnp.int32)
    blocks = pairs.T[:2]
    blocks = blocks % NX * NZ + blocks // NX
    return jnp.sum(pick[None] * blocks[:, None, :], axis=2), ranks


def per_device(spectra, block_counts, pairs):
    table, ranks = plans(pairs, lax.axis_index("chan") % NX)
    return call_kernel(spectra, jnp.asarray(phase_tables()), table, ranks, block_counts)


def solution(mesh):
    placed = (P("tm", "chan", None), P(), P())
    return jax.shard_map(
        per_device, mesh=mesh, in_specs=placed, out_specs=P("chan", "tm", None), check_vma=False
    )
```

time: 958 us -> 192 us (0.20)
  waiting for transfers between devices: 675 us -> 0 us
  Pallas kernels: 0 us -> 186 us
  local copies, waits for them, and re-layouts: 109 us -> 1.63 us
  other arithmetic: 101 us -> 2.41 us
  starting transfers between devices: 31.2 us -> 0 us
  matrix products: 21.4 us -> 0 us
  between operations: 13.6 us -> 0.04 us
    all_to_all x3 -> x0, waiting for transfers between devices: 642 us -> none  [the longest x1 278 us: per_device(): lax.all_to_all(send_target, 'chan', split_axis=0, concat_axis=0, tiled=True)]
    pallas_call x0 -> x1, Pallas kernels: none -> 186 us  [call_kernel(): pl.pallas_call(kernel, out_shape=jax.ShapeDtypeStruct((SLOTS, ROWS, LAGS...]
    unnamed x1 -> x0, other arithmetic: 45.2 us -> none
    convert_element_type x1 -> x0, local copies, waits for them, and re-layouts: 33.3 us -> none  [whiten(): return scaled.astype(jnp.bfloat16).reshape(segs, rows, width)]
    reduce_scatter x1 -> x0, waiting for transfers between devices: 32.6 us -> none  [per_device(): return lax.psum_scatter(results, 'tm', scatter_dimension=1, tiled=True)]
    all_to_all x3 -> x0, starting transfers between devices: 30.9 us -> none  [the longest x1 18.8 us: per_device(): lax.all_to_all(whitened[None], 'chan', split_axis=3, concat_axis=0, tiled...]
    another operation x3 -> x0, other arithmetic: 29.7 us -> none
    dynamic_slice x12 -> x0, local copies, waits for them, and re-layouts: 26.4 us -> none  [the longest x6 19.3 us: one_item(): tgt_one = lax.dynamic_index_in_dim(tgt_all, position, 1, False)]
  transfers between devices with their start and end apart: 4 -> 0, of which waited for: 4 -> 0; matrix products, arithmetic and copies ran while one was open for 2% -> 0% of each run, Pallas kernels for 0% -> 0%
where the time goes in v3:
time: 192 us; the launch traced here: 190 us
  Pallas kernels  186 us (97%)
  other arithmetic  2.41 us (1%)
    pallas_call x1, Pallas kernels, call_kernel(): pl.pallas_call(kernel, out_shape=jax.ShapeDtypeStruct((SLOTS, ROWS, LAGS...  186 us

profile of v3, /device:TPU:6, one launch (start us, length us, event | category | flops | bytes accessed | tf_op | source)
XLA Modules:
  0.0 189.7 jit_solution(12176442841595654935)
XLA Ops:
  0.0 0.7 bitcast_add_fusion
  0.7 0.1 pad_add_fusion
  0.8 0.2 convert_reduce_fusion.ranks
  1.0 0.0 copy-start
  1.0 0.7 fusion.1
  1.7 0.1 compare_convert_fusion
  1.8 0.7 multiply_reduce_fusion.table
  2.5 0.0 copy-done
  2.5 185.6 %stack.1 = f32[3,16,1024]{2,1,0:T(8,128)} custom-call(bf16[1,128,8192]{2,1,0:T(8,128)(2,1)} %spectra.1, f32[16,2,4,8,128]{4,3,2,1,0:T(8,128)} %constant.47.clone.phases, s32[2,24]{1,0:T(2,128)} %multiply_reduce_fusion.table, s32[161]{0:T(256)} %copy-done, s32[64]{0:T(128)} %counts.1), custom_call_target="tpu_custom_call" | custom-call | tf_op jit(solution)/shard_map/stack/pallas_call | solution.py:418
  188.1 1.6 copy.6
  (4 shorter events, 0.0 us)
Async XLA Ops:
  1.0 1.5 copy-start

commit v4 on v3

--- a/solution.py
+++ b/solution.py
@@ -22,7 +22,7 @@
 BANDS = F // BAND // NZ
 WIDE = 2 * BAND
 MINE = NPAIRS // NX
-PIECES = (4, 4, 4, 4, 3, 3, 1, 1)
+PIECES = (2, 2, 3, 3, 3, 3, 4, 4)
 FIRST = tuple(sum(PIECES[:b]) for b in range(len(PIECES)))
 QUAD = 4
 ROWS = 16
@@ -55,7 +55,7 @@
 def kernel(
     spectra, phases, table, ranks, counts, out,
     spec, trig, held0, held1, held2, held3, moved, acc, part, mine, other, h, u, v,
-    sums, sent1, got1, sum2, sent2, got2, final, give, got,
+    sums, sent1, got1, sum2, sent2, got2, final, give, got, spot,
     local, zsend, zrecv, xsend, xrecv, fsend, frecv,
     csend, crecv, ysend, yrecv, send1, recv1, send2, recv2, gsend, grecv,
 ):
@@ -95,14 +95,17 @@
     load_trig.wait()
     alive = (lax.broadcasted_iota(jnp.int32, (BLK, WIDE), 0) < counts[chan]).astype(F32)
 
-    def whiten(i, carry):
-        cols = pl.ds(pl.multiple_of(i * WIDE, WIDE), WIDE)
-        t = spec[:, cols].astype(F32)
-        power = jnp.sum(t * t, axis=-1, keepdims=True) * (1.0 / BAND)
-        spec[:, cols] = (t * lax.rsqrt(power + 1e-06) * alive).astype(BF16)
-        return carry
-
-    lax.fori_loop(0, F // BAND, whiten, 0)
+    def whiten(q):
+        def one(zt, carry):
+            cols = pl.ds(pl.multiple_of((zt * BANDS + q) * WIDE, WIDE), WIDE)
+            t = spec[:, cols].astype(F32)
+            power = jnp.sum(t * t, axis=-1, keepdims=True) * (1.0 / BAND)
+            spec[:, cols] = (t * lax.rsqrt(power + 1e-06) * alive).astype(BF16)
+            return carry
+
+        lax.fori_loop(0, NZ, one, 0)
+
+    whiten(0)
     pl.semaphore_wait(barrier, owners + 2)
 
     def columns(zt, q):
@@ -192,6 +195,17 @@
     for q in range(BANDS):
         own(q).start()
         zsends(q)
+        if q < BANDS - 1:
+            whiten(q + 1)
+
+    def find(o, carry):
+        first = ranks[NPAIRS + o]
+        count = ranks[NPAIRS + o + 1] - first
+        skip = (x + 4 * NPAIRS - first) % NX
+        spot[o] = jnp.where(skip < count, (first + skip) // NX, MINE)
+        return carry
+
+    lax.fori_loop(0, owners, find, 0)
 
     third = MINE // 3
     prev = None
@@ -335,42 +349,39 @@
         swaps(b)
         swaps(b + 1)
 
+    couples = len(PIECES) // 2
     compute(0)
     compute(2)
     both(to_far, 0)
-    compute(4)
-    compute(6)
-    both(to_near, 0)
-    both(to_far, 1)
-    both(to_sums, 0)
-    both(to_near, 1)
-    both(to_far, 2)
-    both(to_far_z, 0)
-    both(to_sums, 1)
-    both(to_near, 2)
-    both(to_far, 3)
-    both(to_far_z, 1)
-    both(to_sums, 2)
-    both(to_near, 3)
-    both(to_far_z, 2)
-    both(to_sums, 3)
-    both(to_far_z, 3)
-    both(to_final, 0, 1, 2, 3)
+    for g in range(2, couples):
+        compute(2 * g)
+    for g in range(couples):
+        both(to_near, g)
+        if g + 1 < couples:
+            both(to_far, g + 1)
+        if g:
+            both(to_far_z, g - 1)
+        both(to_sums, g)
+    both(to_far_z, couples - 1)
+    both(to_final, *range(couples))
     final[MINE] = jnp.zeros((TROW, TCOL), final.dtype)
 
     def fill(o):
-        first = ranks[NPAIRS + o]
-        count = ranks[NPAIRS + o + 1] - first
-        skip = (x + 4 * NPAIRS - first) % NX
-        give[o] = final[jnp.where(skip < count, (first + skip) // NX, MINE)]
-
-    def deliver(d, carry):
-        o = (chan + d) % owners
+        give[o] = final[spot[o]]
+
+    def deliver(k, carry):
+        zt = (z + 8 + (1 - 2 * (k % 2)) * ((k + 1) // 2)) % NZ
+        for xt in range(NX):
+            o = zt * NX + xt
+            fill(o)
+            remote(give.at[o], got.at[chan], gsend, grecv, {"chan": o}).start()
+        return carry
+
+    lax.fori_loop(0, NZ - 1, deliver, 0)
+    for k in range(1, NX):
+        o = z * NX + (x + k) % NX
         fill(o)
         remote(give.at[o], got.at[chan], gsend, grecv, {"chan": o}).start()
-        return carry
-
-    lax.fori_loop(1, owners, deliver, 0)
     fill(chan)
     got[chan] = give[chan]
     many = pl.ds(0, owners - 1)
@@ -441,6 +452,7 @@
             pltpu.VMEM((MINE + 1, TROW, TCOL), BF16),
             pltpu.VMEM((NBLK, TROW, TCOL), BF16),
             pltpu.VMEM((NBLK, TROW, TCOL), BF16),
+            pltpu.SMEM((NBLK,), jnp.int32),
             dma((BANDS + 2,)),
             dma((BANDS,)), dma((BANDS, 5)),
             dma((BANDS, 2)), dma((BANDS, 5, 2)),

time: 192 us -> 183 us (0.953); the launches traced: 190 us -> 183 us
  Pallas kernels: 186 us -> 179 us
    pallas_call x1, Pallas kernels: 186 us -> 179 us  [call_kernel(): pl.pallas_call(kernel, out_shape=jax.ShapeDtypeStruct((SLOTS, ROWS, LAGS...]
where the time goes in v4:
time: 183 us
  Pallas kernels  179 us (98%)
  other arithmetic  2.41 us (1%)
    pallas_call x1, Pallas kernels, call_kernel(): pl.pallas_call(kernel, out_shape=jax.ShapeDtypeStruct((SLOTS, ROWS, LAGS...  179 us

profile of v4, /device:TPU:6, one launch (start us, length us, event | category | flops | bytes accessed | tf_op | source)
XLA Modules:
  0.0 183.2 jit_solution(16476427171106294300)
XLA Ops:
  0.0 0.7 bitcast_add_fusion
  0.7 0.1 pad_add_fusion
  0.8 0.2 convert_reduce_fusion.ranks
  1.0 0.0 copy-start
  1.0 0.7 fusion.1
  1.7 0.1 compare_convert_fusion
  1.8 0.7 multiply_reduce_fusion.table
  2.5 0.0 copy-done
  2.5 179.2 %stack.1 = f32[3,16,1024]{2,1,0:T(8,128)} custom-call(bf16[1,128,8192]{2,1,0:T(8,128)(2,1)} %spectra.1, f32[16,2,4,8,128]{4,3,2,1,0:T(8,128)} %constant.47.clone.phases, s32[2,24]{1,0:T(2,128)} %multiply_reduce_fusion.table, s32[161]{0:T(256)} %copy-done, s32[64]{0:T(128)} %counts.1), custom_call_target="tpu_custom_call" | custom-call | tf_op jit(solution)/shard_map/stack/pallas_call | solution.py:429
  181.6 1.6 copy.6
  (4 shorter events, 0.0 us)
Async XLA Ops:
  1.0 1.5 copy-start

commit v5 on v4

--- a/solution.py
+++ b/solution.py
@@ -84,13 +84,8 @@
     for where in (core, up, down):
         pl.semaphore_signal(barrier, inc=1, device_id=where, device_id_type=MESH)
 
-    def greet(d, carry):
-        pl.semaphore_signal(
-            barrier, inc=1, device_id={"chan": (chan + d) % owners}, device_id_type=MESH
-        )
-        return carry
-
-    lax.fori_loop(1, owners, greet, 0)
+    for where in [right, left, opposite] + [{"chan": (z + d) % NZ * NX + x} for d in range(1, NZ)]:
+        pl.semaphore_signal(barrier, inc=1, device_id=where, device_id_type=MESH)
     load.wait()
     load_trig.wait()
     alive = (lax.broadcasted_iota(jnp.int32, (BLK, WIDE), 0) < counts[chan]).astype(F32)
@@ -106,7 +101,7 @@
         lax.fori_loop(0, NZ, one, 0)
 
     whiten(0)
-    pl.semaphore_wait(barrier, owners + 2)
+    pl.semaphore_wait(barrier, NZ - 1 + 6)
 
     def columns(zt, q):
         return spec.at[:, pl.ds(pl.multiple_of((zt * BANDS + q) * WIDE, WIDE), WIDE)]
@@ -396,7 +391,7 @@
                 t = got[(r * FLAT + l) * NX + group].astype(F32)
                 out[k, r * TROW : (r + 1) * TROW, l * TCOL : (l + 1) * TCOL] = jnp.where(
                     k < count, t, 0.0
-                )
+                ).astype(BF16)
 
     bytes_of(give.at[many], gsend)
     for q in range(BANDS):
@@ -428,7 +423,7 @@
     n = len(PIECES)
     return pl.pallas_call(
         kernel,
-        out_shape=jax.ShapeDtypeStruct((SLOTS, ROWS, LAGS * BLK), F32),
+        out_shape=jax.ShapeDtypeStruct((SLOTS, ROWS, LAGS * BLK), BF16),
         in_specs=[hbm, hbm, smem, smem, smem],
         out_specs=vmem,
         scratch_shapes=[
@@ -493,7 +488,8 @@
 
 def per_device(spectra, block_counts, pairs):
     table, ranks = plans(pairs, lax.axis_index("chan") % NX)
-    return call_kernel(spectra, jnp.asarray(phase_tables()), table, ranks, block_counts)
+    stacks = call_kernel(spectra, jnp.asarray(phase_tables()), table, ranks, block_counts)
+    return stacks.astype(F32)
 
 
 def solution(mesh):

time: 183 us -> 181 us (0.989)
  Pallas kernels: 179 us -> 176 us
    pallas_call x1, Pallas kernels: 179 us -> 176 us  [call_kernel(): pl.pallas_call(kernel, out_shape=jax.ShapeDtypeStruct((SLOTS, ROWS, LAGS...]
where the time goes in v5:
time: 181 us; the launch traced here: 180 us
  Pallas kernels  176 us (97%)
  other arithmetic  3.99 us (2%)
    pallas_call x1, Pallas kernels, call_kernel(): pl.pallas_call(kernel, out_shape=jax.ShapeDtypeStruct((SLOTS, ROWS, LAGS...  176 us

profile of v5, /device:TPU:6, one launch (start us, length us, event | category | flops | bytes accessed | tf_op | source)
XLA Modules:
  0.0 180.3 jit_solution(5178718853899793456)
XLA Ops:
  0.0 0.7 bitcast_add_fusion
  0.7 0.1 pad_add_fusion
  0.8 0.2 convert_reduce_fusion.ranks
  1.0 0.0 copy-start
  1.0 0.7 fusion.1
  1.7 0.1 compare_convert_fusion
  1.8 0.7 multiply_reduce_fusion.table
  2.5 0.0 copy-done
  2.5 176.2 %stack.1 = bf16[3,16,1024]{2,1,0:T(8,128)(2,1)} custom-call(bf16[1,128,8192]{2,1,0:T(8,128)(2,1)} %spectra.1, f32[16,2,4,8,128]{4,3,2,1,0:T(8,128)} %constant.47.clone.phases, s32[2,24]{1,0:T(2,128)} %multiply_reduce_fusion.table, s32[161]{0:T(256)} %copy-done, s32[64]{0:T(128)} %counts.1), custom_call_target="tpu_custom_call" | custom-call | tf_op jit(solution)/shard_map/stack/pallas_call | solution.py:424
  178.7 1.6 convert_element_type.15
  (4 shorter events, 0.0 us)
Async XLA Ops:
  1.0 1.5 copy-start
